TPU v7x, 256 devices: a whole 4x4x8 slice. The times are simulated.
256 devices in a mesh: samp: 64 (over z, x, core), snp: 4 (over y).
Axes of the slice: x: 4, y: 4, z: 8, core: 2. Of those that a mesh axis runs over, the one named last changes fastest.
Arguments:
- genotype: int32 [40960, 4096], P('samp', 'snp'), may hold values from 0 to 2
- freqs: float32 [4096], P('snp'), may hold values from 0.35 to 0.65
- left_factors: float32 [40960, 20], P('samp'), may hold values from -6 to 6
- singular: float32 [20], replicated, may hold values from 0.5 to 2
- right_factors: float32 [4096, 20], P(('snp', 'samp')), may hold values from -1.25 to 1.25
- sketch: bfloat16 [4096, 64], P('snp'), may hold values from -6 to 6
- batch_sizes: int32 [12], replicated, may hold values from 1 to 6826, 40960 in all
- missing_batch: int32 [48], replicated, may hold values from 0 to 11, as said below
- missing_block: int32 [48], replicated, may hold values from 0 to 15, as said below
Outputs:
- basis: float32 [40960, 64], P('samp')
- projection: float32 [4096, 64], P('snp')
- snp_basis: float32 [4096, 64], P('snp')
Inputs may be any that keep to these rules, and one draw needn't show every extreme that they name: The pairs (missing_batch, missing_block) are distinct; every block id appears exactly 3 times and every batch id exactly 48 // 12 times. `missing_block`: paired entry by entry with missing_batch.
All inputs are finite; a program needn't handle non-finite values.
Results may differ from a plain program's by a relative error of at most 0.012.
Values may be sent and summed in bfloat16 or wider, within the bound.
No kernel may reach another device: no remote copies, remote signals or barrier semaphores. Data moves between devices by JAX's collectives and lax.ppermute only.
A program may use at most 64 MiB of HBM per device.

v0:
```python
import math
import jax
import jax.numpy as jnp
from jax import lax
from jax.sharding import PartitionSpec as P

BATCHES = 12
BLOCK = 256
ITERS = 2
BLOCKS = 16


def finish_basis(values, gram):
    lower = jnp.linalg.cholesky(gram)
    return jax.scipy.linalg.solve_triangular(lower, values.T, lower=True).T


def reversed_basis(values, gram):
    flipped = finish_basis(values[:, ::-1], gram[::-1, ::-1])
    return flipped[:, ::-1]


def own_gram(values):
    return jnp.dot(values.T, values, precision=lax.Precision.HIGHEST)


def sample_basis(matrix, right_side, sample_count):
    partial_value = jnp.dot(matrix, right_side, preferred_element_type=jnp.float32)
    summed = lax.psum(partial_value.astype(jnp.bfloat16), "snp").astype(jnp.float32)
    gram = lax.psum(own_gram(summed), "samp") / sample_count
    return finish_basis(summed, gram)


def snp_columns(matrix, basis):
    local_part = lax.dot_general(
        matrix,
        basis.astype(jnp.bfloat16),
        (((0,), (0,)), ((), ())),
        preferred_element_type=jnp.float32,
    )
    return lax.psum(local_part, "samp")


def snp_basis(columns, snp_count):
    gram = lax.psum(own_gram(columns), "snp") / snp_count
    return reversed_basis(columns, gram)


def on_device(
    genotype,
    freqs,
    left_factors,
    singular,
    right_factors,
    sketch,
    batch_sizes,
    missing_batch,
    missing_block,
):
    row_count, col_width = genotype.shape
    sample_count = row_count * lax.axis_size("samp")
    snp_count = col_width * lax.axis_size("snp")
    right_local = lax.all_gather(right_factors, "samp", axis=0, tiled=True)
    batch_range = jnp.arange(BATCHES, dtype=jnp.int32)
    block_range = jnp.arange(BLOCKS, dtype=jnp.int32)
    hot_batch = (missing_batch[:, None] == batch_range[None, :]).astype(jnp.float32)
    hot_block = (missing_block[:, None] == block_range[None, :]).astype(jnp.float32)
    table = jnp.dot(hot_batch.T, hot_block, preferred_element_type=jnp.float32)
    ends = jnp.cumsum(batch_sizes)
    row_ids = lax.axis_index("samp") * row_count + jnp.arange(row_count, dtype=jnp.int32)
    batch_of = jnp.sum((row_ids[:, None] >= ends[None, :]).astype(jnp.int32), axis=1)
    row_hot = (batch_of[:, None] == batch_range[None, :]).astype(jnp.float32)
    col_ids = lax.axis_index("snp") * col_width + jnp.arange(col_width, dtype=jnp.int32)
    col_hot = ((col_ids // BLOCK)[None, :] == block_range[:, None]).astype(jnp.float32)
    missing = (
        jnp.dot(
            jnp.dot(row_hot, table, preferred_element_type=jnp.float32),
            col_hot,
            preferred_element_type=jnp.float32,
        )
        > 0.5
    )
    lowrank = jnp.dot(
        left_factors * singular[None, :], right_local.T, precision=lax.Precision.HIGHEST
    )
    observed = genotype.astype(jnp.float32) - 2.0 * freqs[None, :]
    matrix = jnp.where(missing, lowrank, observed).astype(jnp.bfloat16)
    basis = sample_basis(matrix, sketch, sample_count)
    column_basis = jnp.zeros((col_width, sketch.shape[1]), jnp.float32)
    for sweep_index in range(ITERS):
        column_basis = snp_basis(snp_columns(matrix, basis), snp_count)
        basis = sample_basis(matrix, column_basis.astype(jnp.bfloat16), sample_count)
    projection = snp_columns(matrix, basis) / math.sqrt(sample_count)
    return (basis, projection, column_basis)


def solution(mesh):
    in_specs = (
        P("samp", "snp"),
        P("snp"),
        P("samp", None),
        P(),
        P(("snp", "samp"), None),
        P("snp", None),
        P(),
        P(),
        P(),
    )
    out_specs = (P("samp", None), P("snp", None), P("snp", None))
    return jax.shard_map(
        on_device, mesh=mesh, in_specs=in_specs, out_specs=out_specs, check_vma=False
    )
```

profile of v0, /device:TPU:1, one launch (start us, length us, event | category | flops | bytes accessed | tf_op | source)
XLA Modules:
  0.0 1585.5 jit_solution(2528023982231809789)
XLA Ops:
  7.3 0.7 broadcast_multiply_fusion.6
  8.0 54.6 %all_gather.3 = f32[1024,20]{1,0:T(8,128)S(1)} all-gather(f32[16,20]{1,0:T(8,128)} %param.18), channel_id=1, replica_groups=mesh['samp'=64,'snp'=4] {'samp'}, dimensions={0}, use_global_device_ids=true | all-gather | bytes 83200 | tf_op jit(solution)/shard_map/all_gather | solution.py:63
  62.6 0.8 reduce-window.8
  63.4 0.1 convert_reduce_fusion
  63.5 0.9 fusion.43
  64.4 2.2 fusion
  66.6 5.1 select_convert_fusion
  71.7 1.2 convolution_convert_fusion.2
  72.9 40.8 %all-reduce.7.cloned.1.call-done = bf16[640,64]{0,1:T(8,128)(2,1)} async-done(((bf16[640,64]{0,1:T(8,128)(2,1)}), bf16[640,64]{0,1:T(8,128)(2,1)}) %all-reduce.7.cloned.1.call-update) | async-done | bytes 81936 | tf_op jit(solution)/shard_map/psum | solution.py:29
  113.7 1.1 fusion.49
  114.8 246.0 %psum.78 = f32[64,64]{0,1:T(8,128)S(1)} all-reduce(f32[64,64]{0,1:T(8,128)S(1)} %fusion.49), channel_id=1, replica_groups=mesh['samp'=64,'snp'=4] {'samp'}, use_global_device_ids=true, to_apply=%region_3.4 | all-reduce | flops 4096 | bytes 32768 | tf_op jit(solution)/shard_map/psum | solution.py:30
  360.8 0.1 copy.23
  360.9 5.8 cholesky.89
  366.8 0.6 compare_reduce_fusion.4
  367.4 0.7 fusion.18
  368.1 4.9 custom-call.11
  373.0 1.2 convolution_convert_fusion.4
  374.3 1.1 fusion.54
  375.4 176.2 %all-reduce.9.cloned.1.call-done = f32[1024,64]{0,1:T(8,128)} async-done(((f32[1024,64]{0,1:T(8,128)}), f32[1024,64]{0,1:T(8,128)}) %all-reduce.9.cloned.1.call-update) | async-done | bytes 262160 | tf_op jit(solution)/shard_map/psum | solution.py:41
  551.6 1.4 fusion.50
  553.0 0.1 reverse.6
  553.1 13.3 psum.80
  566.5 5.8 cholesky.100
  572.4 0.6 compare_reduce_fusion.3
  573.0 0.7 fusion.19
  573.7 4.9 custom-call.12
  578.6 3.1 rev.19
  581.6 0.4 convolution_bitcast_fusion.1
  582.1 0.3 rev.20
  582.3 1.2 convolution_convert_fusion.1
  583.5 0.2 all-reduce.13.cloned.1.call-start
  583.7 42.7 %all-reduce.11.cloned.1.call-done = bf16[640,64]{0,1:T(8,128)(2,1)} async-done(((bf16[640,64]{0,1:T(8,128)(2,1)}), bf16[640,64]{0,1:T(8,128)(2,1)}) %all-reduce.11.cloned.1.call-update) | async-done | bytes 81936 | tf_op jit(solution)/shard_map/psum | solution.py:29
  626.4 1.1 fusion.51
  627.5 246.0 %psum.82 = f32[64,64]{0,1:T(8,128)S(1)} all-reduce(f32[64,64]{0,1:T(8,128)S(1)} %fusion.51), channel_id=1, replica_groups=mesh['samp'=64,'snp'=4] {'samp'}, use_global_device_ids=true, to_apply=%region_9.13 | all-reduce | flops 4096 | bytes 32768 | tf_op jit(solution)/shard_map/psum | solution.py:30
  873.6 5.8 cholesky.111
  879.5 0.6 compare_reduce_fusion.2
  880.1 0.7 fusion.20
  880.8 4.9 custom-call.13
  885.7 1.2 convolution_convert_fusion.3
  886.9 1.1 fusion.55
  888.1 176.2 %all-reduce.13.cloned.1.call-done = f32[1024,64]{0,1:T(8,128)} async-done(((f32[1024,64]{0,1:T(8,128)}), f32[1024,64]{0,1:T(8,128)}) %all-reduce.13.cloned.1.call-update) | async-done | bytes 262160 | tf_op jit(solution)/shard_map/psum | solution.py:41
  1064.3 1.4 fusion.52
  1065.7 0.1 reverse.7
  1065.8 13.3 psum.84
  1079.2 5.8 cholesky.122
  1085.1 0.6 compare_reduce_fusion.1
  1085.7 0.7 fusion.21
  1086.4 4.9 custom-call.14
  1091.3 3.1 rev.22
  1094.4 0.4 convolution_bitcast_fusion
  1094.8 0.2 rev.23
  1095.0 1.2 convolution_convert_fusion
  1096.2 42.8 %all-reduce.15.cloned.1.call-done = bf16[640,64]{0,1:T(8,128)(2,1)} async-done(((bf16[640,64]{0,1:T(8,128)(2,1)}), bf16[640,64]{0,1:T(8,128)(2,1)}) %all-reduce.15.cloned.1.call-update) | async-done | bytes 81936 | tf_op jit(solution)/shard_map/psum | solution.py:29
  1139.1 1.1 fusion.53
  1140.2 246.0 %psum.86 = f32[64,64]{0,1:T(8,128)S(1)} all-reduce(f32[64,64]{0,1:T(8,128)S(1)} %fusion.53), channel_id=1, replica_groups=mesh['samp'=64,'snp'=4] {'samp'}, use_global_device_ids=true, to_apply=%region_13.17 | all-reduce | flops 4096 | bytes 32768 | tf_op jit(solution)/shard_map/psum | solution.py:30
  1386.2 0.1 copy.31
  1386.3 5.8 cholesky.133
  1392.2 0.6 compare_reduce_fusion
  1392.8 0.7 fusion.22
  1393.5 4.9 custom-call.15
  1398.4 1.2 convolution_bitcast_fusion.2
  1399.6 1.1 fusion.15
  1400.7 176.2 %all-reduce.17.cloned.1.call-done = f32[1024,64]{0,1:T(8,128)} async-done(((f32[1024,64]{0,1:T(8,128)}), f32[1024,64]{0,1:T(8,128)}) %all-reduce.17.cloned.1.call-update) | async-done | bytes 262160 | tf_op jit(solution)/shard_map/psum | solution.py:41
  1576.9 1.7 broadcast_multiply_fusion
  (41 shorter events, 0.8 us)
Async XLA Ops:
  7.2 64.5 %copy-start = (bf16[1024,64]{0,1:T(8,128)(2,1)S(1)}, bf16[1024,64]{0,1:T(8,128)(2,1)}, u32[]{:S(2)}) copy-start(bf16[1024,64]{0,1:T(8,128)(2,1)} %param.19) | copy-start | bytes 393220
  7.2 106.5 %all-reduce.7.cloned.1.call-start = ((), (), s32[]{:S(2)}) async-start(), calls=%async_computation | async-start | bytes 163840 | tf_op jit(solution)/shard_map/psum | solution.py:29
  64.4 2.2 copy-start.3
  64.4 2.2 copy-start.4
  72.9 478.7 %all-reduce.9.cloned.1.call-start = ((), (), s32[]{:S(2)}) async-start(), calls=%async_computation.1 | async-start | bytes 524288 | tf_op jit(solution)/shard_map/psum | solution.py:41
  375.3 251.1 %all-reduce.11.cloned.1.call-start = ((), (), s32[]{:S(2)}) async-start(), calls=%async_computation.2 | async-start | bytes 163840 | tf_op jit(solution)/shard_map/psum | solution.py:29
  583.5 480.8 %all-reduce.13.cloned.1.call-start = ((), (), s32[]{:S(2)}) async-start(), calls=%async_computation.3 | async-start | bytes 524288 | tf_op jit(solution)/shard_map/psum | solution.py:41
  888.0 251.0 %all-reduce.15.cloned.1.call-start = ((), (), s32[]{:S(2)}) async-start(), calls=%async_computation.4 | async-start | bytes 163840 | tf_op jit(solution)/shard_map/psum | solution.py:29
  1095.0 305.7 %copy-start.1 = (f32[1024,64]{0,1:T(8,128)}, f32[1024,64]{0,1:T(8,128)S(1)}, u32[]{:S(2)}) copy-start(f32[1024,64]{0,1:T(8,128)S(1)} %rev.23) | copy-start | bytes 786436
  1096.2 480.8 %all-reduce.17.cloned.1.call-start = ((), (), s32[]{:S(2)}) async-start(), calls=%async_computation.5 | async-start | bytes 524288 | tf_op jit(solution)/shard_map/psum | solution.py:41
  1399.6 179.0 %copy-start.2 = (f32[640,64]{0,1:T(8,128)}, f32[640,64]{0,1:T(8,128)S(1)}, u32[]{:S(2)}) copy-start(f32[640,64]{0,1:T(8,128)S(1)} %convolution_bitcast_fusion.2) | copy-start | bytes 491524
Sparse Core Ops, SparseCore 0:
  73.0 40.6 all-reduce.6
  375.5 176.0 all-reduce.8
  583.6 42.7 all-reduce.10
  888.2 176.1 all-reduce.12
  1096.3 42.7 all-reduce.14
  1400.8 176.0 all-reduce.16
where the time goes:
time: 1590 us
  blocking collectives  819 us (52%)
  waiting for transfers between devices  655 us (41%)
  other arithmetic  63.7 us (4%)
  matrix products  25.5 us (2%)
    psum x3, blocking collectives, sample_basis(): gram = lax.psum(own_gram(summed), 'samp') / sample_count  738 us
    psum x3, waiting for transfers between devices, snp_columns(): return lax.psum(local_part, 'samp')  529 us
    psum x3, waiting for transfers between devices, sample_basis(): lax.psum(partial_value.astype(jnp.bfloat16), 'snp').astype(jnp.float32)  126 us
    all_gather x1, blocking collectives, on_device(): right_local = lax.all_gather(right_factors, 'samp', axis=0, tiled=True)  54.6 us
    another operation x15, other arithmetic, finish_basis(): lower = jnp.linalg.cholesky(gram)  32.6 us
  transfers between devices with their start and end apart: 6, of which 6 were waited for; matrix products, arithmetic and copies ran while one was open for 0% of the time, Pallas kernels for 0%

commit v1 on v0

--- a/solution.py
+++ b/solution.py
@@ -8,6 +8,12 @@
 BLOCK = 256
 ITERS = 2
 BLOCKS = 16
+
+
+def gather_and_add(value, axis):
+    parts = lax.all_gather(value, axis, axis=0, tiled=False)
+    total = parts.sum(axis=0)
+    return total
 
 
 def finish_basis(values, gram):
@@ -38,7 +44,7 @@
         (((0,), (0,)), ((), ())),
         preferred_element_type=jnp.float32,
     )
-    return lax.psum(local_part, "samp")
+    return gather_and_add(local_part, "samp")
 
 
 def snp_basis(columns, snp_count):

time: 1590 us -> 1440 us (0.906)
  waiting for transfers between devices: 655 us -> 427 us
  local copies, waits for them, and re-layouts: 7.18 us -> 54.4 us
  other arithmetic: 63.7 us -> 88.2 us
    psum x3 -> x0, waiting for transfers between devices: 529 us -> none  [snp_columns(): return lax.psum(local_part, 'samp')]
    all_gather x0 -> x3, waiting for transfers between devices: none -> 302 us  [gather_and_add(): parts = lax.all_gather(value, axis, axis=0, tiled=False)]
    unnamed x10 -> x15, local copies, waits for them, and re-layouts: 0.03 us -> 53.1 us
    reduce_sum x0 -> x3, other arithmetic: none -> 25.4 us  [gather_and_add(): total = parts.sum(axis=0)]
where the time goes in v1:
time: 1440 us; the launch traced here: 1430 us
  blocking collectives  819 us (57%)
  waiting for transfers between devices  427 us (30%)
  other arithmetic  88.2 us (6%)
  local copies, waits for them, and re-layouts  54.4 us (4%)
  matrix products  23.5 us (2%)
  between operations  14.7 us (1%)
    psum x3, blocking collectives, sample_basis(): gram = lax.psum(own_gram(summed), 'samp') / sample_count  738 us
    all_gather x3, waiting for transfers between devices, gather_and_add(): parts = lax.all_gather(value, axis, axis=0, tiled=False)  302 us
    psum x3, waiting for transfers between devices, sample_basis(): lax.psum(partial_value.astype(jnp.bfloat16), 'snp').astype(jnp.float32)  125 us
    all_gather x1, blocking collectives, on_device(): right_local = lax.all_gather(right_factors, 'samp', axis=0, tiled=True)  54.6 us
    unnamed x15, local copies, waits for them, and re-layouts  53.1 us
    another operation x15, other arithmetic, finish_basis(): lower = jnp.linalg.cholesky(gram)  32.6 us
  transfers between devices with their start and end apart: 6, of which 6 were waited for; matrix products, arithmetic and copies ran while one was open for 0% of the time, Pallas kernels for 0%

profile of v1, /device:TPU:1, one launch (start us, length us, event | category | flops | bytes accessed | tf_op | source)
XLA Modules:
  0.0 1428.2 jit_solution(2491156806354644555)
XLA Ops:
  7.3 0.7 broadcast_multiply_fusion.6
  8.0 54.6 %all_gather.21 = f32[1024,20]{1,0:T(8,128)S(1)} all-gather(f32[16,20]{1,0:T(8,128)} %param.18), channel_id=1, replica_groups=mesh['samp'=64,'snp'=4] {'samp'}, dimensions={0}, use_global_device_ids=true | all-gather | bytes 83200 | tf_op jit(solution)/shard_map/all_gather | solution.py:69
  62.6 0.8 reduce-window.8
  63.5 0.9 fusion.43
  64.4 2.3 fusion
  66.7 5.1 select_convert_fusion
  71.8 1.2 convolution_convert_fusion.2
  73.1 40.8 %all-reduce.4.cloned.1.call-done = bf16[640,64]{0,1:T(8,128)(2,1)} async-done(((bf16[640,64]{0,1:T(8,128)(2,1)}), bf16[640,64]{0,1:T(8,128)(2,1)}) %all-reduce.4.cloned.1.call-update) | async-done | bytes 81936 | tf_op jit(solution)/shard_map/psum | solution.py:35
  113.8 1.1 fusion.49
  114.9 246.0 %psum.57 = f32[64,64]{0,1:T(8,128)S(1)} all-reduce(f32[64,64]{0,1:T(8,128)S(1)} %fusion.49), channel_id=1, replica_groups=mesh['samp'=64,'snp'=4] {'samp'}, use_global_device_ids=true, to_apply=%region_3.4 | all-reduce | flops 4096 | bytes 32768 | tf_op jit(solution)/shard_map/psum | solution.py:36
  361.0 5.8 cholesky.89
  366.9 0.6 compare_reduce_fusion.4
  367.6 0.7 fusion.18
  368.2 4.9 custom-call.11
  373.1 1.2 convolution_convert_fusion.4
  374.4 1.1 fusion.54
  375.5 0.5 all-reduce.6.cloned.1.call-start
  376.0 100.3 %all-gather.7.cloned.1.call-done = f32[65536,64]{0,1:T(8,128)} async-done(((f32[1024,64]{0,1:T(8,128)}), f32[65536,64]{0,1:T(8,128)}) %all-gather.7.cloned.1.call-update) | async-done | bytes 16777232 | tf_op jit(solution)/shard_map/all_gather | solution.py:14
  476.3 17.7 %copy.47 = f32[8,8,64,1024]{3,2,1,0:T(8,128)} copy(f32[8,8,64,1024]{3,1,2,0:T(8,128)} %bitcast.105) | data formatting | bytes 33554432
  493.9 8.5 bitcast_reduce_fusion.2
  502.4 0.4 fusion.50
  502.8 0.2 rev.19
  503.1 13.3 psum.58
  516.5 5.8 cholesky.100
  522.3 0.6 compare_reduce_fusion.3
  523.0 0.7 fusion.19
  523.6 4.9 custom-call.12
  528.5 0.4 convolution_bitcast_fusion.1
  529.0 0.3 rev.20
  529.2 1.2 convolution_convert_fusion.1
  530.5 42.3 %all-reduce.6.cloned.1.call-done = bf16[640,64]{0,1:T(8,128)(2,1)} async-done(((bf16[640,64]{0,1:T(8,128)(2,1)}), bf16[640,64]{0,1:T(8,128)(2,1)}) %all-reduce.6.cloned.1.call-update) | async-done | bytes 81936 | tf_op jit(solution)/shard_map/psum | solution.py:35
  572.7 1.1 fusion.51
  573.8 246.0 %psum.60 = f32[64,64]{0,1:T(8,128)S(1)} all-reduce(f32[64,64]{0,1:T(8,128)S(1)} %fusion.51), channel_id=1, replica_groups=mesh['samp'=64,'snp'=4] {'samp'}, use_global_device_ids=true, to_apply=%region_9.13 | all-reduce | flops 4096 | bytes 32768 | tf_op jit(solution)/shard_map/psum | solution.py:36
  820.0 5.8 cholesky.111
  825.8 0.6 compare_reduce_fusion.2
  826.5 0.7 fusion.20
  827.1 4.9 custom-call.13
  832.0 1.2 convolution_convert_fusion.3
  833.3 1.1 fusion.55
  834.4 0.2 all-reduce.8.cloned.1.call-start
  834.6 100.6 %all-gather.9.cloned.1.call-done = f32[65536,64]{0,1:T(8,128)} async-done(((f32[1024,64]{0,1:T(8,128)}), f32[65536,64]{0,1:T(8,128)}) %all-gather.9.cloned.1.call-update) | async-done | bytes 16777232 | tf_op jit(solution)/shard_map/all_gather | solution.py:14
  935.2 17.7 %copy.48 = f32[8,8,64,1024]{3,2,1,0:T(8,128)} copy(f32[8,8,64,1024]{3,1,2,0:T(8,128)} %bitcast.106) | data formatting | bytes 33554432
  952.8 8.5 bitcast_reduce_fusion.1
  961.3 0.4 fusion.52
  962.0 13.3 psum.61
  975.4 5.8 cholesky.122
  981.2 0.6 compare_reduce_fusion.1
  981.9 0.7 fusion.21
  982.5 4.9 custom-call.14
  987.4 0.4 convolution_bitcast_fusion
  988.1 1.2 convolution_convert_fusion
  989.3 42.3 %all-reduce.8.cloned.1.call-done = bf16[640,64]{0,1:T(8,128)(2,1)} async-done(((bf16[640,64]{0,1:T(8,128)(2,1)}), bf16[640,64]{0,1:T(8,128)(2,1)}) %all-reduce.8.cloned.1.call-update) | async-done | bytes 81936 | tf_op jit(solution)/shard_map/psum | solution.py:35
  1031.6 1.1 fusion.53
  1032.7 246.2 %psum.63 = f32[64,64]{0,1:T(8,128)S(1)} all-reduce(f32[64,64]{0,1:T(8,128)S(1)} %fusion.53), channel_id=1, replica_groups=mesh['samp'=64,'snp'=4] {'samp'}, use_global_device_ids=true, to_apply=%region_13.17 | all-reduce | flops 4096 | bytes 32768 | tf_op jit(solution)/shard_map/psum | solution.py:36
  1279.0 5.8 cholesky.133
  1284.9 0.6 compare_reduce_fusion
  1285.5 0.7 fusion.22
  1286.2 4.9 custom-call.15
  1291.1 1.2 convolution_bitcast_fusion.2
  1292.4 1.1 fusion.15
  1293.4 100.8 %all-gather.11.cloned.1.call-done = f32[65536,64]{0,1:T(8,128)} async-done(((f32[1024,64]{0,1:T(8,128)}), f32[65536,64]{0,1:T(8,128)}) %all-gather.11.cloned.1.call-update) | async-done | bytes 16777232 | tf_op jit(solution)/shard_map/all_gather | solution.py:14
  1394.2 17.7 %copy.49 = f32[8,8,64,1024]{3,2,1,0:T(8,128)} copy(f32[8,8,64,1024]{3,1,2,0:T(8,128)} %bitcast.107) | data formatting | bytes 33554432
  1411.9 8.5 bitcast_reduce_fusion
  1420.4 0.7 broadcast_multiply_fusion
  (49 shorter events, 1.5 us)
Async XLA Ops:
  7.2 64.7 %copy-start = (bf16[1024,64]{0,1:T(8,128)(2,1)S(1)}, bf16[1024,64]{0,1:T(8,128)(2,1)}, u32[]{:S(2)}) copy-start(bf16[1024,64]{0,1:T(8,128)(2,1)} %param.19) | copy-start | bytes 393220
  7.2 59.5 %copy-start.5 = (f32[20]{0:T(128)S(1)}, f32[20]{0:T(128)}, u32[]{:S(2)}) copy-start(f32[20]{0:T(128)} %param.17) | copy-start | bytes 244
  7.2 59.5 %copy-start.4 = (f32[640,20]{0,1:T(8,128)S(1)}, f32[640,20]{0,1:T(8,128)}, u32[]{:S(2)}) copy-start(f32[640,20]{0,1:T(8,128)} %param.16) | copy-start | bytes 153604
  7.2 106.6 %all-reduce.4.cloned.1.call-start = ((), (), s32[]{:S(2)}) async-start(), calls=%async_computation | async-start | bytes 163840 | tf_op jit(solution)/shard_map/psum | solution.py:35
  73.0 403.2 %all-gather.7.cloned.1.call-start = ((), (), s32[]{:S(2)}) async-start(), calls=%async_computation.3 | async-start | bytes 17039360 | tf_op jit(solution)/shard_map/all_gather | solution.py:14
  375.5 197.3 %all-reduce.6.cloned.1.call-start = ((), (), s32[]{:S(2)}) async-start(), calls=%async_computation.1 | async-start | bytes 163840 | tf_op jit(solution)/shard_map/psum | solution.py:35
  530.4 404.8 %all-gather.9.cloned.1.call-start = ((), (), s32[]{:S(2)}) async-start(), calls=%async_computation.4 | async-start | bytes 17039360 | tf_op jit(solution)/shard_map/all_gather | solution.py:14
  834.4 197.2 %all-reduce.8.cloned.1.call-start = ((), (), s32[]{:S(2)}) async-start(), calls=%async_computation.2 | async-start | bytes 163840 | tf_op jit(solution)/shard_map/psum | solution.py:35
  988.1 423.8 %copy-start.2 = (f32[1024,64]{0,1:T(8,128)}, f32[1024,64]{0,1:T(8,128)S(1)}, u32[]{:S(2)}) copy-start(f32[1024,64]{0,1:T(8,128)S(1)} %rev.23) | copy-start | bytes 786436
  989.3 405.0 %all-gather.11.cloned.1.call-start = ((), (), s32[]{:S(2)}) async-start(), calls=%async_computation.5 | async-start | bytes 17039360 | tf_op jit(solution)/shard_map/all_gather | solution.py:14
  1292.3 119.6 %copy-start.3 = (f32[640,64]{0,1:T(8,128)}, f32[640,64]{0,1:T(8,128)S(1)}, u32[]{:S(2)}) copy-start(f32[640,64]{0,1:T(8,128)S(1)} %convolution_bitcast_fusion.2) | copy-start | bytes 491524
  1411.9 9.2 copy-start.1
Sparse Core Ops, SparseCore 0:
  73.1 40.6 all-reduce.3
  375.6 100.6 all-gather.6
  530.5 42.1 all-reduce.5
  834.5 100.6 all-gather.8
  989.4 42.1 all-reduce.7
  1293.6 100.6 all-gather.10
